TPU v7x, 32 devices: a whole 2x2x4 slice. The times are simulated.
32 devices in a mesh: ens: 2 (over x), lat: 4 (over y, core), lon: 4 (over z).
Axes of the slice: x: 2, y: 2, z: 4, core: 2. Of those that a mesh axis runs over, the one named last changes fastest.
Arguments:
- starting_state: bfloat16 [4, 222, 128, 512], P('ens', None, 'lat', 'lon'), may hold values from -6 to 6
- random_fields: bfloat16 [4, 16, 128, 512], P('ens', None, 'lat', 'lon'), may hold values from -6 to 6
- observed: float32 [6, 13, 128, 512], P(None, None, 'lat', 'lon'), may hold values from -6 to 6
- input_weight: bfloat16 [256, 222], replicated, may hold values from -0.375 to 0.375
- random_weight: bfloat16 [256, 16], replicated, may hold values from -1.5 to 1.5
- hidden_weight: bfloat16 [256, 256], replicated, may hold values from -0.375 to 0.375
- output_weight: bfloat16 [222, 256], replicated, may hold values from -0.375 to 0.375
- diffusivity: float32 [222], replicated, may hold values from 0.02 to 0.24
Outputs:
- grad_state: bfloat16 [4, 222, 128, 512], P('ens', None, 'lat', 'lon')
- grad_w_in: float32 [256, 222], replicated
- grad_w_noise: float32 [256, 16], replicated
- grad_w_mid: float32 [256, 256], replicated
- grad_w_out: float32 [222, 256], replicated
- grad_diffusivity: float32 [222], replicated
All inputs are finite; a program needn't handle non-finite values.
Results may differ from a plain program's by a relative error of at most 0.008.
Values may be sent and summed in bfloat16 or wider, within the bound.
No kernel may reach another device: no remote copies, remote signals or barrier semaphores. Data moves between devices by JAX's collectives and lax.ppermute only.
A program may use at most 128 MiB of HBM per device.

v0:
```python
import jax
import jax.numpy as jnp
from jax import lax
from jax.sharding import PartitionSpec as P

PROGNOSTIC_COUNT = 6
LEVEL_COUNT = 37
SCORED = 13
DELTA = 0.1


def with_halo(block, sides, width):
    for axis, dim in sides:
        count = lax.axis_size(axis)
        forward = [(i, i + 1) for i in range(count - 1)]
        forward.append((count - 1, 0))
        backward = [(target, source) for source, target in forward]
        low = lax.ppermute(
            lax.slice_in_dim(block, block.shape[dim] - width, None, axis=dim), axis, forward
        )
        high = lax.ppermute(lax.slice_in_dim(block, 0, width, axis=dim), axis, backward)
        block = jnp.concatenate([low, block, high], axis=dim)
    return block


def softened_slope(diff):
    return diff * lax.rsqrt(diff * diff + DELTA * DELTA)


def silu_slope(value):
    gate = jax.nn.sigmoid(value)
    return gate * (1.0 + value * (1.0 - gate))


def pole_mask(padded):
    lat_id = lax.axis_index("lat")
    lat_count = lax.axis_size("lat")
    row_ids = jnp.arange(padded.shape[2])
    dropped = (row_ids == 0) & (lat_id == 0) | (row_ids == padded.shape[2] - 1) & (
        lat_id == lat_count - 1
    )
    return padded * jnp.logical_not(dropped)[:, None].astype(padded.dtype)


def stencil(padded, field):
    return (
        padded[:, :, 2:, 1:-1]
        + padded[:, :, :-2, 1:-1]
        + padded[:, :, 1:-1, 2:]
        + padded[:, :, 1:-1, :-2]
        - 4.0 * field
    )


def on_device(
    starting_state,
    random_fields,
    observed,
    input_weight,
    random_weight,
    hidden_weight,
    output_weight,
    diffusivity,
):
    resident_members, channels, latitude_rows, longitude_columns = starting_state.shape
    cells = latitude_rows * longitude_columns
    hidden_width = hidden_weight.shape[0]
    evaluated_rows = PROGNOSTIC_COUNT * SCORED
    padded_state = pole_mask(with_halo(starting_state, (("lat", 2), ("lon", 3)), 1))
    start = starting_state.astype(jnp.float32)
    laplacian_initial = stencil(padded_state.astype(jnp.float32), start)
    stepped = start + diffusivity[None, :, None, None] * laplacian_initial
    advanced_partner = stepped.astype(jnp.bfloat16).reshape(resident_members, channels, cells)
    random_flattened = random_fields.reshape(resident_members, random_fields.shape[1], cells)
    first_preactivation = jnp.einsum(
        "hc,mcn->mhn", input_weight, advanced_partner, preferred_element_type=jnp.float32
    )
    first_preactivation = first_preactivation + jnp.einsum(
        "hk,mkn->mhn", random_weight, random_flattened, preferred_element_type=jnp.float32
    )
    first_activation = jax.nn.silu(first_preactivation).astype(jnp.bfloat16)
    second_preactivation = jnp.einsum(
        "hk,mkn->mhn", hidden_weight, first_activation, preferred_element_type=jnp.float32
    )
    second_activation = jax.nn.silu(second_preactivation).astype(jnp.bfloat16)
    w_out_scored = output_weight.reshape(PROGNOSTIC_COUNT, LEVEL_COUNT, hidden_width)[
        :, ::3
    ].reshape(evaluated_rows, hidden_width)
    advanced_evaluated = stepped.reshape(resident_members, PROGNOSTIC_COUNT, LEVEL_COUNT, cells)[
        :, :, ::3
    ].reshape(resident_members, evaluated_rows, cells)
    member_prediction = advanced_evaluated + jnp.einsum(
        "ch,mhn->mcn", w_out_scored, second_activation, preferred_element_type=jnp.float32
    )
    member_prediction = member_prediction.astype(jnp.bfloat16).reshape(
        resident_members, evaluated_rows, latitude_rows, longitude_columns
    )
    observed_target = observed.reshape(evaluated_rows, latitude_rows, longitude_columns)
    own_values = member_prediction.astype(jnp.float32)
    shard_values = lax.all_gather(member_prediction, "ens", axis=0, tiled=True).astype(jnp.float32)

    def accumulate_member(member_index, running):
        partner_member = lax.dynamic_index_in_dim(shard_values, member_index, 0, keepdims=False)
        return running + softened_slope(own_values - partner_member)

    pairwise_sum = lax.fori_loop(
        0, shard_values.shape[0], accumulate_member, jnp.zeros_like(own_values)
    )
    member_count = resident_members * lax.axis_size("ens")
    score_gradient = (
        softened_slope(own_values - observed_target[None]) - pairwise_sum / (member_count - 1.0)
    ).astype(jnp.bfloat16)
    grad_flat = score_gradient.reshape(resident_members, evaluated_rows, cells)
    out_term = jnp.einsum(
        "mcn,mhn->ch", grad_flat, second_activation, preferred_element_type=jnp.float32
    )
    back_second = jnp.einsum(
        "ch,mcn->mhn", w_out_scored, grad_flat, preferred_element_type=jnp.float32
    )
    delta_second = (back_second * silu_slope(second_preactivation)).astype(jnp.bfloat16)
    mid_term = jnp.einsum(
        "mhn,mkn->hk", delta_second, first_activation, preferred_element_type=jnp.float32
    )
    back_first = jnp.einsum(
        "hk,mhn->mkn", hidden_weight, delta_second, preferred_element_type=jnp.float32
    )
    delta_first = (back_first * silu_slope(first_preactivation)).astype(jnp.bfloat16)
    in_term = jnp.einsum(
        "mhn,mcn->hc", delta_first, advanced_partner, preferred_element_type=jnp.float32
    )
    noise_term = jnp.einsum(
        "mhn,mkn->hk", delta_first, random_flattened, preferred_element_type=jnp.float32
    )
    grad_stepped = jnp.einsum(
        "hc,mhn->mcn", input_weight, delta_first, preferred_element_type=jnp.float32
    )
    grad_stepped = (
        grad_stepped.reshape(resident_members, PROGNOSTIC_COUNT, LEVEL_COUNT, cells)
        .at[:, :, ::3]
        .add(
            grad_flat.astype(jnp.float32).reshape(resident_members, PROGNOSTIC_COUNT, SCORED, cells)
        )
    )
    grad_stepped = grad_stepped.reshape(
        resident_members, channels, latitude_rows, longitude_columns
    )
    diffusivity_term = jnp.sum(grad_stepped * laplacian_initial, axis=(0, 2, 3))
    in_term, noise_term, mid_term, out_term, diffusivity_term = lax.psum(
        (in_term, noise_term, mid_term, out_term, diffusivity_term), ("ens", "lat", "lon")
    )
    padded_grad = pole_mask(
        with_halo(grad_stepped.astype(jnp.bfloat16), (("lat", 2), ("lon", 3)), 1).astype(
            grad_stepped.dtype
        )
    )
    grad_laplace = stencil(padded_grad, grad_stepped)
    grad_state = (grad_stepped + diffusivity[None, :, None, None] * grad_laplace).astype(
        jnp.bfloat16
    )
    inverse_count = 1.0 / (
        resident_members
        * lax.axis_size("ens")
        * latitude_rows
        * lax.axis_size("lat")
        * longitude_columns
        * lax.axis_size("lon")
    )
    grad_w_out = (
        jnp.zeros((PROGNOSTIC_COUNT, LEVEL_COUNT, hidden_width), jnp.float32)
        .at[:, ::3]
        .set(out_term.reshape(PROGNOSTIC_COUNT, SCORED, hidden_width))
        .reshape(channels, hidden_width)
    )
    return (
        grad_state,
        in_term * inverse_count,
        noise_term * inverse_count,
        mid_term * inverse_count,
        grad_w_out * inverse_count,
        diffusivity_term * inverse_count,
    )


def solution(mesh):
    in_specs = (
        P("ens", None, "lat", "lon"),
        P("ens", None, "lat", "lon"),
        P(None, None, "lat", "lon"),
        P(),
        P(),
        P(),
        P(),
        P(),
    )
    out_specs = (P("ens", None, "lat", "lon"), P(), P(), P(), P(), P())
    return jax.shard_map(
        on_device, mesh=mesh, in_specs=in_specs, out_specs=out_specs, check_vma=False
    )
```

profile of v0, /device:TPU:0, one launch (start us, length us, event | category | flops | bytes accessed | tf_op | source)
XLA Modules:
  0.0 457.5 jit_solution(17218860512130126049)
XLA Ops:
  7.2 1.9 fusion.34
  9.7 2.0 collective-permute-start.1
  11.7 1.1 reshape.82
  12.8 5.2 %fusion.27 = f32[2,4096,256]{2,1,0:T(8,128)} fusion(bf16[2,16,4096]{2,1,0:T(8,128)(2,1)S(1)} %reshape.82, bf16[256,16]{0,1:T(8,128)(2,1)} %param.14), kind=kOutput, calls=%fused_computation.67 | convolution fusion | flops 67108864 | bytes 8658944 | tf_op jit(solution)/shard_map/hk,mkn->mhn/dot_general | solution.py:78
  18.0 8.3 %copy.76 = bf16[2,222,32,128]{1,2,3,0:T(8,128)(2,1)} copy(bf16[2,222,32,128]{3,2,1,0:T(8,128)(2,1)} %param.10) | data formatting | bytes 7274496 | tf_op args[0]
  26.7 0.8 pad_maximum_fusion.5
  27.5 2.4 collective-permute-start.2
  29.9 2.4 collective-permute-start.3
  32.5 1.6 collective-permute-done.2
  34.5 4.8 %fusion.19 = f32[2,222,34,130]{1,2,3,0:T(8,128)S(1)} fusion(bf16[2,222,34,1]{1,2,3,0:T(8,128)(2,1)S(1)} %collective-permute-done.3, bf16[2,222,1,128]{1,2,3,0:T(2,128)(2,1)S(1)} %copy.81, bf16[2,222,32,128]{1,2,3,0:T(8,128)(2,1)} %copy.76, bf16[2,222,1,128]{1,2,3,0:T(2,128)(2,1)S(1)} %copy.79, bf16[2,222,34,1]{1,2,3,0:T(8,128)(2,1)S(1)} %collective-permute-done.2, ...), kind=kLoop, calls=%fused_computation.44 | loop fusion | flops 23549760 | bytes 11774948 | tf_op jit(solution)/shard_map/convert_element_type | solution.py:71
  39.3 11.2 %fusion.31 = (bf16[2,222,32,128]{1,2,3,0:T(8,128)(2,1)}, f32[2,222,32,128]{1,2,3,0:T(8,128)}, f32[2,222,32,128]{1,2,3,0:T(8,128)}) fusion(f32[222]{0:T(256)S(1)} %copy-done.10, bf16[2,222,32,128]{1,2,3,0:T(8,128)(2,1)} %copy.76, f32[2,222,34,130]{1,2,3,0:T(8,128)S(1)} %fusion.19), kind=kLoop, calls=%fused_computation.75 | loop fusion | flops 16367616 | bytes 50922360 | tf_op jit(solution)/shard_map/convert_element_type | solution.py:73
  50.5 8.3 %copy.83 = bf16[2,222,32,128]{3,2,1,0:T(8,128)(2,1)} copy(bf16[2,222,32,128]{1,2,3,0:T(8,128)(2,1)} %get-tuple-element.126) | data formatting | bytes 7274496 | tf_op jit(solution)/shard_map/convert_element_type | solution.py:73
  58.8 4.4 reshape.81
  63.2 10.1 %copy.82 = f32[2,222,32,128]{3,2,0,1:T(8,128)} copy(f32[2,222,32,128]{1,2,3,0:T(8,128)} %get-tuple-element.127) | data formatting | bytes 14548992 | tf_op jit(solution)/shard_map/add | solution.py:72
  73.3 10.0 %reshape.79 = f32[2,6,37,4096]{3,0,2,1:T(2,128)} reshape(f32[2,222,32,128]{3,2,0,1:T(8,128)} %copy.82) | data formatting | bytes 14548992 | tf_op jit(solution)/shard_map/reshape | solution.py:89
  83.3 2.0 slice.62
  85.4 9.0 %fusion.16 = (bf16[2,256,4096]{1,2,0:T(8,128)(2,1)S(1)}, f32[2,4096,256]{2,1,0:T(8,128)}) fusion(f32[2,4096,256]{2,1,0:T(8,128)} %fusion.27, bf16[2,222,4096]{2,1,0:T(8,128)(2,1)} %reshape.81, bf16[256,222]{0,1:T(8,128)(2,1)S(1)} %copy-done.8), kind=kOutput, calls=%fused_computation.37 | convolution fusion | flops 943718400 | bytes 24722432 | tf_op jit(solution)/shard_map/hc,mcn->mhn/dot_general | solution.py:75
  94.4 4.7 %fusion.10 = (bf16[2,256,4096]{1,2,0:T(8,128)(2,1)S(1)}, f32[2,4096,256]{2,1,0:T(8,128)}) fusion(bf16[2,256,4096]{1,2,0:T(8,128)(2,1)S(1)} %get-tuple-element.139, bf16[256,256]{1,0:T(8,128)(2,1)S(1)} %copy-done), kind=kOutput, calls=%fused_computation.28 | convolution fusion | flops 1084227584 | bytes 16908288 | tf_op jit(solution)/shard_map/hk,mkn->mhn/dot_general | solution.py:82
  99.1 2.0 copy-done.3
  101.1 2.0 fusion.21
  103.1 1.6 reshape.85
  105.3 3.2 convert_element_type.74
  108.5 36.1 %all-gather.2.cloned.1.call-done = bf16[4,78,32,128]{3,2,1,0:T(8,128)(2,1)} async-done(((bf16[2,78,32,128]{3,2,1,0:T(8,128)(2,1)}), bf16[4,78,32,128]{3,2,1,0:T(8,128)(2,1)}) %all-gather.2.cloned.1.call-update) | async-done | bytes 2555920 | tf_op jit(solution)/shard_map/all_gather | solution.py:100
  144.6 4.8 %convert_element_type.75 = f32[4,78,32,128]{3,2,1,0:T(8,128)} convert(bf16[4,78,32,128]{3,2,1,0:T(8,128)(2,1)} %all-gather.2.cloned.1.call-done) | non-fusion elementwise | flops 1277952 | bytes 7667712 | tf_op jit(solution)/shard_map/convert_element_type | solution.py:100
  149.4 24.0 %while.14 = (s32[]{:T(128)}, f32[2,78,32,128]{3,2,1,0:T(8,128)}, f32[4,78,32,128]{3,2,1,0:T(8,128)}, f32[2,78,32,128]{3,2,1,0:T(8,128)}, s32[]{:T(128)}, /*index=5*/s32[]{:T(128)}) while((s32[]{:T(128)}, f32[2,78,32,128]{3,2,1,0:T(8,128)}, f32[4,78,32,128]{3,2,1,0:T(8,128)}, f32[2,78,32,128]{3,2,1,0:T(8,128)}, s32[]{:T(128)}, ...), condition=%wide.region_1.2_spmd.clone, body=%wide.region_0.1_spmd.clone.sunk | while | flops 3833859 | bytes 11501651 | solution.py:106
  149.4 1.5 dynamic-slice_bitcast_fusion.2
  150.9 4.0 select_add_fusion.2
  154.9 1.4 dynamic-slice_bitcast_fusion.2
  156.3 4.8 %select_add_fusion.2 = f32[2,78,32,128]{3,2,1,0:T(8,128)} fusion(f32[2,78,32,128]{3,2,1,0:T(8,128)} %get-tuple-element.175, f32[2,78,32,128]{3,2,1,0:T(8,128)} %get-tuple-element.183, f32[78,32,128]{2,1,0:T(8,128)S(1)} %dynamic-slice_bitcast_fusion.2, pred[]{:T(512)S(6)} %compare.3), kind=kLoop, calls=%fused_computation.2.clone.1 | loop fusion | flops 3833856 | bytes 8945665 | tf_op jit(solution)/shard_map/while/body/eval_jaxpr/add | solution.py:104
  161.1 1.4 dynamic-slice_bitcast_fusion.2
  162.5 4.8 %select_add_fusion.2 = f32[2,78,32,128]{3,2,1,0:T(8,128)} fusion(f32[2,78,32,128]{3,2,1,0:T(8,128)} %get-tuple-element.175, f32[2,78,32,128]{3,2,1,0:T(8,128)} %get-tuple-element.183, f32[78,32,128]{2,1,0:T(8,128)S(1)} %dynamic-slice_bitcast_fusion.2, pred[]{:T(512)S(6)} %compare.3), kind=kLoop, calls=%fused_computation.2.clone.1 | loop fusion | flops 3833856 | bytes 8945665 | tf_op jit(solution)/shard_map/while/body/eval_jaxpr/add | solution.py:104
  167.3 1.4 dynamic-slice_bitcast_fusion.2
  168.7 4.8 %select_add_fusion.2 = f32[2,78,32,128]{3,2,1,0:T(8,128)} fusion(f32[2,78,32,128]{3,2,1,0:T(8,128)} %get-tuple-element.175, f32[2,78,32,128]{3,2,1,0:T(8,128)} %get-tuple-element.183, f32[78,32,128]{2,1,0:T(8,128)S(1)} %dynamic-slice_bitcast_fusion.2, pred[]{:T(512)S(6)} %compare.3), kind=kLoop, calls=%fused_computation.2.clone.1 | loop fusion | flops 3833856 | bytes 8945665 | tf_op jit(solution)/shard_map/while/body/eval_jaxpr/add | solution.py:104
  173.4 2.8 subtract_convert_fusion
  177.0 3.2 convolution_bitcast_fusion.4
  180.2 6.4 %fusion.6 = bf16[2,256,4096]{1,2,0:T(8,128)(2,1)S(1)} fusion(f32[2,4096,256]{2,1,0:T(8,128)} %get-tuple-element.142, bf16[2,78,4096]{2,1,0:T(8,128)(2,1)S(1)} %reshape.86, bf16[78,256,1]{1,0,2:T(8,128)(2,1)S(1)} %reshape.110), kind=kOutput, calls=%fused_computation.21 | convolution fusion | flops 346030080 | bytes 13900800 | tf_op jit(solution)/shard_map/ch,mcn->mhn/dot_general | solution.py:117
  186.6 2.0 convolution_bitcast_fusion.2
  188.6 3.5 fusion.5
  192.2 1.8 convolution_bitcast_fusion.3
  194.0 4.4 convolution_bitcast_fusion
  198.4 1.8 copy.88
  200.9 11.8 %copy.87 = f32[2,222,4096]{2,0,1:T(2,128)} copy(f32[2,222,4096]{2,1,0:T(8,128)} %convolution_bitcast_fusion) | data formatting | bytes 14548992 | tf_op jit(solution)/shard_map/hc,mhn->mcn/transpose | solution.py:134
  212.7 2.4 reshape.92
  215.1 1.9 copy.89
  217.0 16.4 %scatter_fusion = f32[2,6,37,4096]{3,0,2,1:T(2,128)} fusion(f32[2,6,37,4096]{3,0,2,1:T(2,128)} %bitcast.129, s32[13]{0:T(128)S(1)} %multiply_bitcast_fusion, f32[13,2,6,4096]{3,1,2,0:T(2,128)S(1)} %copy.89), kind=kCustom, calls=%fused_computation | custom fusion | flops 638976 | bytes 7667764 | tf_op jit(solution)/shard_map/scatter-add | solution.py:140
  233.4 10.9 %reshape.88 = f32[2,222,32,128]{3,2,0,1:T(8,128)} reshape(f32[2,6,37,4096]{3,0,2,1:T(2,128)} %scatter_fusion) | data formatting | bytes 14548992 | tf_op jit(solution)/shard_map/reshape | solution.py:144
  244.3 10.1 %copy.96 = f32[2,222,32,128]{1,2,3,0:T(8,128)} copy(f32[2,222,32,128]{3,2,0,1:T(8,128)} %reshape.88) | data formatting | bytes 14548992 | tf_op jit(solution)/shard_map/reshape | solution.py:144
  254.4 10.2 %multiply_reduce_fusion = (f32[222]{0:T(256)S(1)}, bf16[2,222,32,128]{1,2,3,0:T(8,128)(2,1)S(1)}) fusion(f32[2,222,32,128]{1,2,3,0:T(8,128)} %copy.96, f32[2,222,32,128]{1,2,3,0:T(8,128)} %get-tuple-element.128), kind=kLoop, calls=%fused_computation.40 | loop fusion | flops 5455650 | bytes 18187128 | tf_op jit(solution)/shard_map/reduce_sum | solution.py:147
  264.6 2.0 copy-done.1
  267.4 1.8 collective-permute-start.5
  269.2 39.4 %all-reduce = (f32[256,16]{0,1:T(8,128)S(1)}, f32[222]{0:T(256)S(1)}) all-reduce(f32[256,16]{0,1:T(8,128)S(1)} %convolution_bitcast_fusion.5, f32[222]{0:T(256)S(1)} %get-tuple-element.129), channel_id=1, replica_groups=mesh['ens'=2,'lat'=4,'lon'=4] {'ens','lat','lon'}, use_global_device_ids=true, to_apply=%region_4.5 | all-reduce | flops 4318 | bytes 34544 | tf_op jit(solution)/shard_map/psum | solution.py:148
  309.6 0.8 pad_maximum_fusion.2
  310.5 1.5 collective-permute-start.6
  312.0 2.4 collective-permute-start.7
  314.9 0.7 copy.102
  315.6 0.8 collective-permute-done.6
  316.4 8.6 %convert_multiply_fusion = f32[2,222,34,130]{1,2,3,0:T(8,128)} fusion(bf16[2,222,34,1]{1,2,3,0:T(8,128)(2,1)S(1)} %collective-permute-done.7, bf16[2,222,1,128]{1,2,3,0:T(2,128)(2,1)S(1)} %copy.94, bf16[2,222,32,128]{1,2,3,0:T(8,128)(2,1)} %copy-done.1, bf16[2,222,1,128]{1,2,3,0:T(2,128)(2,1)S(1)} %copy.93, ...), kind=kLoop, calls=%fused_computation.4 | loop fusion | flops 21587280 | bytes 11775016 | tf_op jit(solution)/shard_map/mul | solution.py:42
  325.0 19.3 %fusion.4 = bf16[2,222,32,128]{1,2,3,0:T(8,128)(2,1)} fusion(f32[2,222,32,128]{1,2,3,0:T(8,128)} %copy.96, f32[2,222,34,130]{1,2,3,0:T(8,128)} %convert_multiply_fusion, f32[222]{0:T(256)S(1)} %copy-done.10), kind=kLoop, calls=%fused_computation.12 | loop fusion | flops 14548992 | bytes 40010616 | tf_op jit(solution)/shard_map/convert_element_type | solution.py:157
  344.3 8.3 %copy.105 = bf16[2,222,32,128]{3,2,1,0:T(8,128)(2,1)} copy(bf16[2,222,32,128]{1,2,3,0:T(8,128)(2,1)} %fusion.4) | data formatting | bytes 7274496
  352.6 92.1 %all-reduce.4.cloned.1.call-done = (f32[256,222]{0,1:T(8,128)}, f32[256,256]{1,0:T(8,128)}, f32[6,13,256]{2,0,1:T(8,128)}) async-done(((f32[256,222]{0,1:T(8,128)}, f32[256,256]{1,0:T(8,128)}, f32[6,13,256]{2,0,1:T(8,128)}), (f32[256,222]{0,1:T(8,128)}, f32[256,256]{1,0:T(8,128)}, f32[6,13,256]{2,0,1:T(8,128)})) %all-reduce.4.cloned.1.call-update) | async-done | bytes 569360 | tf_op jit(solution)/shard_map/psum | solution.py:148
  444.7 1.7 scatter_fusion.1
  446.4 0.7 mul.158
  447.2 1.7 broadcast_multiply_fusion
  448.8 1.6 broadcast_multiply_fusion.1
  (60 shorter events, 6.1 us)
Async XLA Ops:
  7.2 87.2 %copy-start = (bf16[256,256]{1,0:T(8,128)(2,1)S(1)}, bf16[256,256]{1,0:T(8,128)(2,1)}, u32[]{:S(2)}) copy-start(bf16[256,256]{1,0:T(8,128)(2,1)} %param.15) | copy-start | bytes 393220
  7.2 137.4 %all-gather.2.cloned.1.call-start = ((), (), s32[]{:S(2)}) async-start(), calls=%async_computation | async-start | bytes 3833856 | tf_op jit(solution)/shard_map/all_gather | solution.py:100
  9.1 17.2 %collective-permute-start = (bf16[2,222,1,128]{3,1,2,0:T(8,128)(2,1)S(1)}, bf16[2,222,1,128]{3,1,2,0:T(8,128)(2,1)S(1)}, u32[]{:S(2)}, u32[]{:S(2)}) collective-permute-start(bf16[2,222,1,128]{3,1,2,0:T(8,128)(2,1)S(1)} %copy.113), channel_id=1, source_target_pairs={{0,4},{4,8},{8,12},{12,0},{1,5},{5,9},{9,13},{13,1},{2,6},{6,10},{... | collective-permute-start | bytes 341000 | tf_op jit(solution)/shard_map/ppermute | solution.py:18
  9.7 16.8 %collective-permute-start.1 = (bf16[2,222,1,128]{3,1,2,0:T(8,128)(2,1)S(1)}, bf16[2,222,1,128]{3,1,2,0:T(8,128)(2,1)S(1)}, u32[]{:S(2)}, u32[]{:S(2)}) collective-permute-start(bf16[2,222,1,128]{3,1,2,0:T(8,128)(2,1)S(1)} %copy.114), channel_id=1, source_target_pairs={{4,0},{8,4},{12,8},{0,12},{5,1},{9,5},{13,9},{1,13},{6,2},{10,6},{... | collective-permute-start | bytes 341000 | tf_op jit(solution)/shard_map/ppermute | solution.py:21
  18.0 14.3 %copy-start.9 = (bf16[222,256]{1,0:T(8,128)(2,1)S(1)}, bf16[222,256]{1,0:T(8,128)(2,1)}, u32[]{:S(2)}) copy-start(bf16[222,256]{1,0:T(8,128)(2,1)} %param.16) | copy-start | bytes 340996
  27.5 6.5 %collective-permute-start.2 = (bf16[2,222,34,1]{1,2,3,0:T(8,128)(2,1)S(1)}, bf16[2,222,34,1]{1,2,3,0:T(8,128)(2,1)S(1)}, u32[]{:S(2)}, u32[]{:S(2)}) collective-permute-start(bf16[2,222,34,1]{1,2,3,0:T(8,128)(2,1)S(1)} %get-tuple-element.133), channel_id=1, source_target_pairs={{0,1},{1,2},{2,3},{3,0},{4,5},{5,6},{6,7},{7,4},{8,9},{9,10},{10,1... | collective-permute-start | bytes 90584 | tf_op jit(solution)/shard_map/ppermute | solution.py:18
  29.9 4.5 collective-permute-start.3
  32.4 6.8 %copy-start.10 = (f32[222]{0:T(256)S(1)}, f32[222]{0:T(256)}, u32[]{:S(2)}) copy-start(f32[222]{0:T(256)} %param.17) | copy-start | bytes 2668
  73.3 12.0 %copy-start.8 = (bf16[256,222]{0,1:T(8,128)(2,1)S(1)}, bf16[256,222]{0,1:T(8,128)(2,1)}, u32[]{:S(2)}) copy-start(bf16[256,222]{0,1:T(8,128)(2,1)} %param.13) | copy-start | bytes 340996
  94.4 4.7 %copy-start.4 = (bf16[2,256,4096]{1,2,0:T(8,128)(2,1)}, bf16[2,256,4096]{1,2,0:T(8,128)(2,1)S(1)}, u32[]{:S(2)}) copy-start(bf16[2,256,4096]{1,2,0:T(8,128)(2,1)S(1)} %get-tuple-element.139) | copy-start | bytes 12582916
  99.1 2.0 copy-start.3
  104.7 339.9 %all-reduce.4.cloned.1.call-start = ((), (), s32[]{:S(2)}) async-start(), calls=%async_computation.1 | async-start | bytes 1196032 | tf_op jit(solution)/shard_map/psum | solution.py:148
  149.4 24.0 %copy-start.2 = (bf16[2,78,32,128]{3,2,1,0:T(8,128)(2,1)S(1)}, bf16[2,78,32,128]{3,2,1,0:T(8,128)(2,1)}, u32[]{:S(2)}) copy-start(bf16[2,78,32,128]{3,2,1,0:T(8,128)(2,1)} %reshape.85) | copy-start | bytes 3833860
  177.0 11.7 %slice-start = ((s8[8388608]{0:T(1024)(128)(4,1)}), s8[4194304]{0:T(1024)(128)(4,1)S(1)}, s32[]{:S(2)}) async-start(s8[8388608]{0:T(1024)(128)(4,1)} %bitcast.134), calls=%async_computation.2 | async-start | bytes 8388608
  180.2 6.5 %copy-start.5 = (bf16[2,256,4096]{1,2,0:T(8,128)(2,1)S(1)}, bf16[2,256,4096]{1,2,0:T(8,128)(2,1)}, u32[]{:S(2)}) copy-start(bf16[2,256,4096]{1,2,0:T(8,128)(2,1)} %copy-done.4) | copy-start | bytes 12582916
  180.2 8.5 %slice-start.1 = ((s8[8388608]{0:T(1024)(128)(4,1)}), s8[4194304]{0:T(1024)(128)(4,1)S(1)}, s32[]{:S(2)}) async-start(s8[8388608]{0:T(1024)(128)(4,1)} %bitcast.134), calls=%async_computation.3 | async-start | bytes 8388608
  188.6 3.6 copy-start.7
  200.9 11.8 %copy-start.6 = (f32[2,78,32,128]{3,2,0,1:T(8,128)S(1)}, f32[2,78,32,128]{3,2,0,1:T(8,128)}, u32[]{:S(2)}) copy-start(f32[2,78,32,128]{3,2,0,1:T(8,128)} %copy.88) | copy-start | bytes 7667716
  264.6 2.0 copy-start.1
  267.2 42.1 %collective-permute-start.4 = (bf16[2,222,1,128]{3,1,2,0:T(8,128)(2,1)S(1)}, bf16[2,222,1,128]{3,1,2,0:T(8,128)(2,1)S(1)}, u32[]{:S(2)}, u32[]{:S(2)}) collective-permute-start(bf16[2,222,1,128]{3,1,2,0:T(8,128)(2,1)S(1)} %copy.91), channel_id=1, source_target_pairs={{0,4},{4,8},{8,12},{12,0},{1,5},{5,9},{9,13},{13,1},{2,6},{6,10},{... | collective-permute-start | bytes 341000 | tf_op jit(solution)/shard_map/ppermute | solution.py:18
  267.4 42.0 %collective-permute-start.5 = (bf16[2,222,1,128]{3,1,2,0:T(8,128)(2,1)S(1)}, bf16[2,222,1,128]{3,1,2,0:T(8,128)(2,1)S(1)}, u32[]{:S(2)}, u32[]{:S(2)}) collective-permute-start(bf16[2,222,1,128]{3,1,2,0:T(8,128)(2,1)S(1)} %copy.92), channel_id=1, source_target_pairs={{4,0},{8,4},{12,8},{0,12},{5,1},{9,5},{13,9},{1,13},{6,2},{10,6},{... | collective-permute-start | bytes 341000 | tf_op jit(solution)/shard_map/ppermute | solution.py:21
  310.5 6.0 %collective-permute-start.6 = (bf16[2,222,34,1]{1,2,3,0:T(8,128)(2,1)S(1)}, bf16[2,222,34,1]{1,2,3,0:T(8,128)(2,1)S(1)}, u32[]{:S(2)}, u32[]{:S(2)}) collective-permute-start(bf16[2,222,34,1]{1,2,3,0:T(8,128)(2,1)S(1)} %get-tuple-element.131), channel_id=1, source_target_pairs={{0,1},{1,2},{2,3},{3,0},{4,5},{5,6},{6,7},{7,4},{8,9},{9,10},{10,1... | collective-permute-start | bytes 90584 | tf_op jit(solution)/shard_map/ppermute | solution.py:18
  312.0 4.4 collective-permute-start.7
Sparse Core Ops, SparseCore 0:
  104.9 39.6 all-gather.1
  315.8 128.8 all-reduce.3
where the time goes:
time: 463 us; the launch traced here: 458 us
  waiting for transfers between devices  131 us (28%)
  local copies, waits for them, and re-layouts  110 us (24%)
  other arithmetic  106 us (23%)
  matrix products  43 us (9%)
  blocking collectives  39.4 us (9%)
  between operations  14.6 us (3%)
  starting transfers between devices  13.7 us (3%)
    psum x1, waiting for transfers between devices, on_device(): lax.psum((in_term, noise_term, mid_term, out_term, diffusivity_term), ('e...  92.1 us
    psum x1, blocking collectives, on_device(): lax.psum((in_term, noise_term, mid_term, out_term, diffusivity_term), ('e...  39.4 us
    all_gather x1, waiting for transfers between devices, on_device(): lax.all_gather(member_prediction, 'ens', axis=0, tiled=True)  36.1 us
    reshape x2, local copies, waits for them, and re-layouts, on_device(): grad_stepped.reshape(resident_members, channels, latitude_rows, longitude...  20.9 us
    unnamed x30, local copies, waits for them, and re-layouts  20.7 us
    convert_element_type x1, other arithmetic, on_device(): (grad_stepped + diffusivity[None, :, None, None] * grad_laplace).astype(j...  19.3 us
    add x4, other arithmetic, accumulate_member(): return running + softened_slope(own_values - partner_member)  18.3 us
    scatter-add x1, other arithmetic, on_device(): grad_stepped = grad_stepped.reshape(resident_members, PROGNOSTIC_COUNT, L...  16.4 us
  transfers between devices with their start and end apart: 10, of which 5 were waited for; matrix products, arithmetic and copies ran while one was open for 12% of the time, Pallas kernels for 0%

commit v1 on v0

--- a/solution.py
+++ b/solution.py
@@ -146,7 +146,10 @@
     )
     diffusivity_term = jnp.sum(grad_stepped * laplacian_initial, axis=(0, 2, 3))
     in_term, noise_term, mid_term, out_term, diffusivity_term = lax.psum(
-        (in_term, noise_term, mid_term, out_term, diffusivity_term), ("ens", "lat", "lon")
+        lax.psum(
+            (in_term, noise_term, mid_term, out_term, diffusivity_term), axis_name=("lat", "lon")
+        ),
+        axis_name="ens",
     )
     padded_grad = pole_mask(
         with_halo(grad_stepped.astype(jnp.bfloat16), (("lat", 2), ("lon", 3)), 1).astype(

time: 463 us -> 489 us (1.056)
  blocking collectives: 39.4 us -> 68 us
  waiting for transfers between devices: 131 us -> 123 us
    psum x1 -> x2, blocking collectives: 39.4 us -> 68 us  [the longest x1 60.7 us: on_device(): lax.psum((in_term, noise_term, mid_term, out_term, diffusivity_term), axi...]
    psum x1 -> x2, waiting for transfers between devices: 92.1 us -> 84 us  [the longest x1 80.8 us: on_device(): lax.psum((in_term, noise_term, mid_term, out_term, diffusivity_term), axi...]
    unnamed x30 -> x34, local copies, waits for them, and re-layouts: 20.7 us -> 22.7 us
  transfers between devices with their start and end apart: 10 -> 11, of which waited for: 5 -> 6; matrix products, arithmetic and copies ran while one was open for 12% -> 12% of each run, Pallas kernels for 0% -> 0%
where the time goes in v1:
time: 489 us; the launch traced here: 484 us
  waiting for transfers between devices  123 us (25%)
  local copies, waits for them, and re-layouts  113 us (23%)
  other arithmetic  106 us (22%)
  blocking collectives  68 us (14%)
  matrix products  45.9 us (9%)
  between operations  14.3 us (3%)
  starting transfers between devices  13.7 us (3%)
    psum x1, waiting for transfers between devices, on_device(): lax.psum((in_term, noise_term, mid_term, out_term, diffusivity_term), axi...  80.8 us
    psum x1, blocking collectives, on_device(): lax.psum((in_term, noise_term, mid_term, out_term, diffusivity_term), axi...  60.7 us
    all_gather x1, waiting for transfers between devices, on_device(): lax.all_gather(member_prediction, 'ens', axis=0, tiled=True)  36 us
    unnamed x34, local copies, waits for them, and re-layouts  22.7 us
    reshape x2, local copies, waits for them, and re-layouts, on_device(): grad_stepped.reshape(resident_members, channels, latitude_rows, longitude...  20.9 us
    convert_element_type x1, other arithmetic, on_device(): (grad_stepped + diffusivity[None, :, None, None] * grad_laplace).astype(j...  19.4 us
    add x4, other arithmetic, accumulate_member(): return running + softened_slope(own_values - partner_member)  18.3 us
    scatter-add x1, other arithmetic, on_device(): grad_stepped = grad_stepped.reshape(resident_members, PROGNOSTIC_COUNT, L...  16.4 us
  transfers between devices with their start and end apart: 11, of which 6 were waited for; matrix products, arithmetic and copies ran while one was open for 12% of the time, Pallas kernels for 0%

profile of v1, /device:TPU:0, one launch (start us, length us, event | category | flops | bytes accessed | tf_op | source)
XLA Modules:
  0.0 484.3 jit_solution(15133351573015286691)
XLA Ops:
  7.2 1.9 fusion.34
  9.7 2.0 collective-permute-start.1
  11.7 1.1 reshape.82
  12.8 5.2 %fusion.27 = f32[2,4096,256]{2,1,0:T(8,128)} fusion(bf16[2,16,4096]{2,1,0:T(8,128)(2,1)S(1)} %reshape.82, bf16[256,16]{0,1:T(8,128)(2,1)} %param.14), kind=kOutput, calls=%fused_computation.67 | convolution fusion | flops 67108864 | bytes 8658944 | tf_op jit(solution)/shard_map/hk,mkn->mhn/dot_general | solution.py:78
  18.0 8.3 %copy.76 = bf16[2,222,32,128]{1,2,3,0:T(8,128)(2,1)} copy(bf16[2,222,32,128]{3,2,1,0:T(8,128)(2,1)} %param.10) | data formatting | bytes 7274496 | tf_op args[0]
  26.7 0.8 pad_maximum_fusion.5
  27.5 2.4 collective-permute-start.2
  29.9 2.4 collective-permute-start.3
  32.5 1.6 collective-permute-done.2
  34.5 4.8 fusion.19
  39.3 11.3 %fusion.31 = (bf16[2,222,32,128]{1,2,3,0:T(8,128)(2,1)}, f32[2,222,32,128]{1,2,3,0:T(8,128)}, f32[2,222,32,128]{1,2,3,0:T(8,128)}) fusion(f32[222]{0:T(256)S(1)} %copy-done.12, bf16[2,222,32,128]{1,2,3,0:T(8,128)(2,1)} %copy.76, f32[2,222,34,130]{1,2,3,0:T(8,128)S(1)} %fusion.19), kind=kLoop, calls=%fused_computation.75 | loop fusion | flops 16367616 | bytes 50922360 | tf_op jit(solution)/shard_map/convert_element_type | solution.py:73
  50.6 8.3 %copy.83 = bf16[2,222,32,128]{3,2,1,0:T(8,128)(2,1)} copy(bf16[2,222,32,128]{1,2,3,0:T(8,128)(2,1)} %get-tuple-element.131) | data formatting | bytes 7274496 | tf_op jit(solution)/shard_map/convert_element_type | solution.py:73
  58.8 4.4 reshape.81
  63.3 10.1 %copy.82 = f32[2,222,32,128]{3,2,0,1:T(8,128)} copy(f32[2,222,32,128]{1,2,3,0:T(8,128)} %get-tuple-element.132) | data formatting | bytes 14548992 | tf_op jit(solution)/shard_map/add | solution.py:72
  73.4 10.0 %reshape.79 = f32[2,6,37,4096]{3,0,2,1:T(2,128)} reshape(f32[2,222,32,128]{3,2,0,1:T(8,128)} %copy.82) | data formatting | bytes 14548992 | tf_op jit(solution)/shard_map/reshape | solution.py:89
  83.3 2.0 slice.62
  85.4 9.0 %fusion.16 = (bf16[2,256,4096]{1,2,0:T(8,128)(2,1)S(1)}, f32[2,4096,256]{2,1,0:T(8,128)}) fusion(f32[2,4096,256]{2,1,0:T(8,128)} %fusion.27, bf16[2,222,4096]{2,1,0:T(8,128)(2,1)} %reshape.81, bf16[256,222]{0,1:T(8,128)(2,1)S(1)} %copy-done.10), kind=kOutput, calls=%fused_computation.37 | convolution fusion | flops 943718400 | bytes 24722432 | tf_op jit(solution)/shard_map/hc,mcn->mhn/dot_general | solution.py:75
  94.4 4.7 fusion.10
  99.1 2.0 copy-done.3
  101.1 2.0 fusion.21
  103.1 1.6 reshape.85
  105.4 3.2 convert_element_type.74
  108.5 36.0 %all-gather.2.cloned.1.call-done = bf16[4,78,32,128]{3,2,1,0:T(8,128)(2,1)} async-done(((bf16[2,78,32,128]{3,2,1,0:T(8,128)(2,1)}), bf16[4,78,32,128]{3,2,1,0:T(8,128)(2,1)}) %all-gather.2.cloned.1.call-update) | async-done | bytes 2555920 | tf_op jit(solution)/shard_map/all_gather | solution.py:100
  144.6 4.8 convert_element_type.75
  149.4 24.0 %while.14 = (s32[]{:T(128)}, f32[2,78,32,128]{3,2,1,0:T(8,128)}, f32[4,78,32,128]{3,2,1,0:T(8,128)}, f32[2,78,32,128]{3,2,1,0:T(8,128)}, s32[]{:T(128)}, /*index=5*/s32[]{:T(128)}) while((s32[]{:T(128)}, f32[2,78,32,128]{3,2,1,0:T(8,128)}, f32[4,78,32,128]{3,2,1,0:T(8,128)}, f32[2,78,32,128]{3,2,1,0:T(8,128)}, s32[]{:T(128)}, ...), condition=%wide.region_1.2_spmd.clone, body=%wide.region_0.1_spmd.clone.sunk | while | flops 3833859 | bytes 11501651 | solution.py:106
  149.4 1.5 dynamic-slice_bitcast_fusion.2
  150.9 4.0 select_add_fusion.2
  154.9 1.4 dynamic-slice_bitcast_fusion.2
  156.3 4.8 select_add_fusion.2
  161.1 1.4 dynamic-slice_bitcast_fusion.2
  162.5 4.8 select_add_fusion.2
  167.3 1.4 dynamic-slice_bitcast_fusion.2
  168.7 4.8 select_add_fusion.2
  173.4 2.8 subtract_convert_fusion
  177.0 3.8 convolution_bitcast_fusion.4
  180.8 6.4 %fusion.6 = bf16[2,256,4096]{1,2,0:T(8,128)(2,1)S(1)} fusion(f32[2,4096,256]{2,1,0:T(8,128)} %get-tuple-element.147, bf16[2,78,4096]{2,1,0:T(8,128)(2,1)S(1)} %reshape.86, bf16[78,256,1]{1,0,2:T(8,128)(2,1)S(1)} %reshape.110), kind=kOutput, calls=%fused_computation.21 | convolution fusion | flops 346030080 | bytes 13900800 | tf_op jit(solution)/shard_map/ch,mcn->mhn/dot_general | solution.py:117
  187.2 2.0 convolution_bitcast_fusion.2
  189.3 3.5 fusion.5
  192.8 1.9 copy-done.4
  194.7 1.8 convolution_bitcast_fusion.3
  196.6 6.8 %convolution_bitcast_fusion = f32[2,222,4096]{2,1,0:T(8,128)} fusion(bf16[2,256,4096]{1,2,0:T(8,128)(2,1)} %copy-done.4, bf16[256,222]{0,1:T(8,128)(2,1)S(1)} %copy-done.10), kind=kOutput, calls=%fused_computation.42 | convolution fusion | flops 931135488 | bytes 11582464 | tf_op jit(solution)/shard_map/hc,mhn->mcn/dot_general | solution.py:134
  203.3 1.8 copy.88
  205.8 11.8 %copy.87 = f32[2,222,4096]{2,0,1:T(2,128)} copy(f32[2,222,4096]{2,1,0:T(8,128)} %convolution_bitcast_fusion) | data formatting | bytes 14548992 | tf_op jit(solution)/shard_map/hc,mhn->mcn/transpose | solution.py:134
  217.6 2.4 reshape.92
  220.0 1.9 copy.89
  221.9 16.4 %scatter_fusion = f32[2,6,37,4096]{3,0,2,1:T(2,128)} fusion(f32[2,6,37,4096]{3,0,2,1:T(2,128)} %bitcast.129, s32[13]{0:T(128)S(1)} %multiply_bitcast_fusion, f32[13,2,6,4096]{3,1,2,0:T(2,128)S(1)} %copy.89), kind=kCustom, calls=%fused_computation | custom fusion | flops 638976 | bytes 7667764 | tf_op jit(solution)/shard_map/scatter-add | solution.py:140
  238.4 10.9 %reshape.88 = f32[2,222,32,128]{3,2,0,1:T(8,128)} reshape(f32[2,6,37,4096]{3,0,2,1:T(2,128)} %scatter_fusion) | data formatting | bytes 14548992 | tf_op jit(solution)/shard_map/reshape | solution.py:144
  249.2 10.1 %copy.96 = f32[2,222,32,128]{1,2,3,0:T(8,128)} copy(f32[2,222,32,128]{3,2,0,1:T(8,128)} %reshape.88) | data formatting | bytes 14548992 | tf_op jit(solution)/shard_map/reshape | solution.py:144
  259.3 10.2 %multiply_reduce_fusion = (f32[222]{0:T(256)S(1)}, bf16[2,222,32,128]{1,2,3,0:T(8,128)(2,1)S(1)}) fusion(f32[2,222,32,128]{1,2,3,0:T(8,128)} %copy.96, f32[2,222,32,128]{1,2,3,0:T(8,128)} %get-tuple-element.133), kind=kLoop, calls=%fused_computation.40 | loop fusion | flops 5455650 | bytes 18187128 | tf_op jit(solution)/shard_map/reduce_sum | solution.py:147
  269.5 2.0 copy-done.1
  272.4 1.8 collective-permute-start.5
  274.1 60.7 %all-reduce = (f32[256,16]{0,1:T(8,128)S(1)}, f32[222]{0:T(256)S(1)}) all-reduce(f32[256,16]{0,1:T(8,128)S(1)} %convolution_bitcast_fusion.5, f32[222]{0:T(256)S(1)} %get-tuple-element.134), channel_id=1, replica_groups=mesh['ens'=2,'lat'=4,'lon'=4] {'lat','lon'}, use_global_device_ids=true, to_apply=%region_5.6 | all-reduce | flops 4318 | bytes 34544 | tf_op jit(solution)/shard_map/psum | solution.py:149
  334.8 7.3 %all-reduce.2 = (f32[256,16]{0,1:T(8,128)S(1)}, f32[222]{0:T(256)S(1)}) all-reduce(f32[256,16]{0,1:T(8,128)S(1)} %get-tuple-element.121, f32[222]{0:T(256)S(1)} %get-tuple-element.122), channel_id=1, replica_groups=mesh['ens'=2,'lat'=4,'lon'=4] {'ens'}, use_global_device_ids=true, to_apply=%region_6.7 | all-reduce | flops 4318 | bytes 34544 | tf_op jit(solution)/shard_map/psum | solution.py:148
  344.0 3.8 collective-permute-start.7
  348.5 1.3 collective-permute-done.6
  349.8 8.6 %convert_multiply_fusion = f32[2,222,34,130]{1,2,3,0:T(8,128)} fusion(bf16[2,222,34,1]{1,2,3,0:T(8,128)(2,1)S(1)} %collective-permute-done.7, bf16[2,222,1,128]{1,2,3,0:T(2,128)(2,1)S(1)} %copy.94, bf16[2,222,32,128]{1,2,3,0:T(8,128)(2,1)} %copy-done.1, bf16[2,222,1,128]{1,2,3,0:T(2,128)(2,1)S(1)} %copy.93, ...), kind=kLoop, calls=%fused_computation.4 | loop fusion | flops 21587280 | bytes 11775016 | tf_op jit(solution)/shard_map/mul | solution.py:42
  358.4 80.8 %all-reduce.7.cloned.1.call-done = (f32[256,222]{0,1:T(8,128)}, f32[256,256]{1,0:T(8,128)}, f32[78,256]{1,0:T(8,128)}) async-done(((f32[256,222]{0,1:T(8,128)}, f32[256,256]{1,0:T(8,128)}, f32[78,256]{1,0:T(8,128)}), (f32[256,222]{0,1:T(8,128)}, f32[256,256]{1,0:T(8,128)}, f32[78,256]{1,0:T(8,128)})) %all-reduce.7.cloned.1.call-update) | async-done | bytes 569360 | tf_op jit(solution)/shard_map/psum | solution.py:149
  439.2 0.9 reshape.89
  440.8 19.4 %fusion.4 = bf16[2,222,32,128]{1,2,3,0:T(8,128)(2,1)} fusion(f32[2,222,32,128]{1,2,3,0:T(8,128)} %copy.96, f32[2,222,34,130]{1,2,3,0:T(8,128)} %convert_multiply_fusion, f32[222]{0:T(256)S(1)} %copy-done.12), kind=kLoop, calls=%fused_computation.12 | loop fusion | flops 14548992 | bytes 40010616 | tf_op jit(solution)/shard_map/convert_element_type | solution.py:160
  460.2 8.3 %copy.105 = bf16[2,222,32,128]{3,2,1,0:T(8,128)(2,1)} copy(bf16[2,222,32,128]{1,2,3,0:T(8,128)(2,1)} %fusion.4) | data formatting | bytes 7274496
  468.6 3.1 all-reduce.9.cloned.1.call-done
  471.7 1.7 scatter_fusion.1
  474.2 1.7 broadcast_multiply_fusion
  475.9 1.6 broadcast_multiply_fusion.1
  (68 shorter events, 8.4 us)
Async XLA Ops:
  7.2 87.3 %copy-start = (bf16[256,256]{1,0:T(8,128)(2,1)S(1)}, bf16[256,256]{1,0:T(8,128)(2,1)}, u32[]{:S(2)}) copy-start(bf16[256,256]{1,0:T(8,128)(2,1)} %param.15) | copy-start | bytes 393220
  7.2 137.4 %all-gather.2.cloned.1.call-start = ((), (), s32[]{:S(2)}) async-start(), calls=%async_computation | async-start | bytes 3833856 | tf_op jit(solution)/shard_map/all_gather | solution.py:100
  9.1 17.2 %collective-permute-start = (bf16[2,222,1,128]{3,1,2,0:T(8,128)(2,1)S(1)}, bf16[2,222,1,128]{3,1,2,0:T(8,128)(2,1)S(1)}, u32[]{:S(2)}, u32[]{:S(2)}) collective-permute-start(bf16[2,222,1,128]{3,1,2,0:T(8,128)(2,1)S(1)} %copy.113), channel_id=1, source_target_pairs={{0,4},{4,8},{8,12},{12,0},{1,5},{5,9},{9,13},{13,1},{2,6},{6,10},{... | collective-permute-start | bytes 341000 | tf_op jit(solution)/shard_map/ppermute | solution.py:18
  9.7 16.8 %collective-permute-start.1 = (bf16[2,222,1,128]{3,1,2,0:T(8,128)(2,1)S(1)}, bf16[2,222,1,128]{3,1,2,0:T(8,128)(2,1)S(1)}, u32[]{:S(2)}, u32[]{:S(2)}) collective-permute-start(bf16[2,222,1,128]{3,1,2,0:T(8,128)(2,1)S(1)} %copy.114), channel_id=1, source_target_pairs={{4,0},{8,4},{12,8},{0,12},{5,1},{9,5},{13,9},{1,13},{6,2},{10,6},{... | collective-permute-start | bytes 341000 | tf_op jit(solution)/shard_map/ppermute | solution.py:21
  18.0 14.3 %copy-start.11 = (bf16[222,256]{1,0:T(8,128)(2,1)S(1)}, bf16[222,256]{1,0:T(8,128)(2,1)}, u32[]{:S(2)}) copy-start(bf16[222,256]{1,0:T(8,128)(2,1)} %param.16) | copy-start | bytes 340996
  27.5 6.5 %collective-permute-start.2 = (bf16[2,222,34,1]{1,2,3,0:T(8,128)(2,1)S(1)}, bf16[2,222,34,1]{1,2,3,0:T(8,128)(2,1)S(1)}, u32[]{:S(2)}, u32[]{:S(2)}) collective-permute-start(bf16[2,222,34,1]{1,2,3,0:T(8,128)(2,1)S(1)} %get-tuple-element.138), channel_id=1, source_target_pairs={{0,1},{1,2},{2,3},{3,0},{4,5},{5,6},{6,7},{7,4},{8,9},{9,10},{10,1... | collective-permute-start | bytes 90584 | tf_op jit(solution)/shard_map/ppermute | solution.py:18
  29.9 4.5 collective-permute-start.3
  32.4 6.8 %copy-start.12 = (f32[222]{0:T(256)S(1)}, f32[222]{0:T(256)}, u32[]{:S(2)}) copy-start(f32[222]{0:T(256)} %param.17) | copy-start | bytes 2668
  73.4 12.0 %copy-start.10 = (bf16[256,222]{0,1:T(8,128)(2,1)S(1)}, bf16[256,222]{0,1:T(8,128)(2,1)}, u32[]{:S(2)}) copy-start(bf16[256,222]{0,1:T(8,128)(2,1)} %param.13) | copy-start | bytes 340996
  94.4 4.7 copy-start.6
  99.1 2.0 copy-start.3
  104.8 334.5 %all-reduce.7.cloned.1.call-start = ((), (), s32[]{:S(2)}) async-start(), calls=%async_computation.1 | async-start | bytes 1146880 | tf_op jit(solution)/shard_map/psum | solution.py:149
  149.4 24.0 %copy-start.2 = (bf16[2,78,32,128]{3,2,1,0:T(8,128)(2,1)S(1)}, bf16[2,78,32,128]{3,2,1,0:T(8,128)(2,1)}, u32[]{:S(2)}) copy-start(bf16[2,78,32,128]{3,2,1,0:T(8,128)(2,1)} %reshape.85) | copy-start | bytes 3833860
  177.0 12.3 %slice-start = ((s8[8388608]{0:T(1024)(128)(4,1)}), s8[4194304]{0:T(1024)(128)(4,1)S(1)}, s32[]{:S(2)}) async-start(s8[8388608]{0:T(1024)(128)(4,1)} %bitcast.134), calls=%async_computation.3 | async-start | bytes 8388608
  180.8 6.4 %copy-start.7 = (bf16[2,256,4096]{1,2,0:T(8,128)(2,1)S(1)}, bf16[2,256,4096]{1,2,0:T(8,128)(2,1)}, u32[]{:S(2)}) copy-start(bf16[2,256,4096]{1,2,0:T(8,128)(2,1)} %copy-done.6) | copy-start | bytes 12582916
  180.8 8.4 %slice-start.1 = ((s8[8388608]{0:T(1024)(128)(4,1)}), s8[4194304]{0:T(1024)(128)(4,1)S(1)}, s32[]{:S(2)}) async-start(s8[8388608]{0:T(1024)(128)(4,1)} %bitcast.134), calls=%async_computation.4 | async-start | bytes 8388608
  189.2 5.5 %copy-start.9 = (bf16[2,222,4096]{2,1,0:T(8,128)(2,1)S(1)}, bf16[2,222,4096]{2,1,0:T(8,128)(2,1)}, u32[]{:S(2)}) copy-start(bf16[2,222,4096]{2,1,0:T(8,128)(2,1)} %reshape.81) | copy-start | bytes 10911748
  192.8 1.9 copy-start.4
  196.6 8.6 %copy-start.5 = (bf16[2,256,4096]{1,2,0:T(8,128)(2,1)S(1)}, bf16[2,256,4096]{1,2,0:T(8,128)(2,1)}, u32[]{:S(2)}) copy-start(bf16[2,256,4096]{1,2,0:T(8,128)(2,1)} %copy-done.4) | copy-start | bytes 12582916
  205.8 11.8 %copy-start.8 = (f32[2,78,32,128]{3,2,0,1:T(8,128)S(1)}, f32[2,78,32,128]{3,2,0,1:T(8,128)}, u32[]{:S(2)}) copy-start(f32[2,78,32,128]{3,2,0,1:T(8,128)} %copy.88) | copy-start | bytes 7667716
  269.5 2.0 copy-start.1
  272.1 70.6 %collective-permute-start.4 = (bf16[2,222,1,128]{3,1,2,0:T(8,128)(2,1)S(1)}, bf16[2,222,1,128]{3,1,2,0:T(8,128)(2,1)S(1)}, u32[]{:S(2)}, u32[]{:S(2)}) collective-permute-start(bf16[2,222,1,128]{3,1,2,0:T(8,128)(2,1)S(1)} %copy.91), channel_id=1, source_target_pairs={{0,4},{4,8},{8,12},{12,0},{1,5},{5,9},{9,13},{13,1},{2,6},{6,10},{... | collective-permute-start | bytes 341000 | tf_op jit(solution)/shard_map/ppermute | solution.py:18
  272.4 70.6 %collective-permute-start.5 = (bf16[2,222,1,128]{3,1,2,0:T(8,128)(2,1)S(1)}, bf16[2,222,1,128]{3,1,2,0:T(8,128)(2,1)S(1)}, u32[]{:S(2)}, u32[]{:S(2)}) collective-permute-start(bf16[2,222,1,128]{3,1,2,0:T(8,128)(2,1)S(1)} %copy.92), channel_id=1, source_target_pairs={{4,0},{8,4},{12,8},{0,12},{5,1},{9,5},{13,9},{1,13},{6,2},{10,6},{... | collective-permute-start | bytes 341000 | tf_op jit(solution)/shard_map/ppermute | solution.py:21
  344.0 5.9 %collective-permute-start.6 = (bf16[2,222,34,1]{1,2,3,0:T(8,128)(2,1)S(1)}, bf16[2,222,34,1]{1,2,3,0:T(8,128)(2,1)S(1)}, u32[]{:S(2)}, u32[]{:S(2)}) collective-permute-start(bf16[2,222,34,1]{1,2,3,0:T(8,128)(2,1)S(1)} %get-tuple-element.136), channel_id=1, source_target_pairs={{0,1},{1,2},{2,3},{3,0},{4,5},{5,6},{6,7},{7,4},{8,9},{9,10},{10,1... | collective-permute-start | bytes 90584 | tf_op jit(solution)/shard_map/ppermute | solution.py:18
  344.0 5.8 %collective-permute-start.7 = (bf16[2,222,34,1]{1,2,3,0:T(8,128)(2,1)S(1)}, bf16[2,222,34,1]{1,2,3,0:T(8,128)(2,1)S(1)}, u32[]{:S(2)}, u32[]{:S(2)}) collective-permute-start(bf16[2,222,34,1]{1,2,3,0:T(8,128)(2,1)S(1)} %get-tuple-element.137), channel_id=1, source_target_pairs={{1,0},{2,1},{3,2},{0,3},{5,4},{6,5},{7,6},{4,7},{9,8},{10,9},{11,1... | collective-permute-start | bytes 90584 | tf_op jit(solution)/shard_map/ppermute | solution.py:21
  348.4 123.3 %all-reduce.9.cloned.1.call-start = ((), (), s32[]{:S(2)}) async-start(), calls=%async_computation.2 | async-start | bytes 1196032 | tf_op jit(solution)/shard_map/psum | solution.py:148
Sparse Core Ops, SparseCore 0:
  104.9 39.6 all-gather.1
  348.6 90.6 all-reduce.6
  442.3 29.3 all-reduce.8
